TPU v7x, 256 devices: a whole 4x4x8 slice. The times are simulated.
256 devices in a mesh: dp: 32 (over z_hi, y, core), tensor: 8 (over x, z_lo).
Axes of the slice: x: 4, y: 4, z: 8 (z_hi: 4, z_lo: 2; z = z_hi * 2 + z_lo), core: 2. Of those that a mesh axis runs over, the one named last changes fastest.
Arguments:
- hidden: bfloat16 [32, 1024, 28672], P('dp', None, 'tensor'), may hold values from -6 to 6
- grad_out: bfloat16 [32, 1024, 8192], P('dp', None, 'tensor'), may hold values from -30 to 30
- proj_in: bfloat16 [64, 28672], P(None, 'tensor'), may hold values from -0.03125 to 0.03125
- proj_out: bfloat16 [64, 8192], P(None, 'tensor'), may hold values from -0.0625 to 0.0625
Outputs:
- covariance: float32 [4096, 4096], P('dp', 'tensor')
All inputs are finite; a program needn't handle non-finite values.
Results may differ from a plain program's by a relative error of at most 0.0003.
Values sent between devices are 32-bit elements; how exact they have to be, the bound alone decides.
No kernel may reach another device: no remote copies, remote signals or barrier semaphores. Data moves between devices by JAX's collectives and lax.ppermute only.
A program may use at most 64 MiB of HBM per device.

v0:
```python
import math

import jax
import jax.numpy as jnp
from jax import lax
from jax.sharding import PartitionSpec as P


def outer_sum(panels, width):
    left_side = panels[:, :, :width]
    right_side = panels[:, :, width:]
    return jnp.einsum(
        "sta,stb->sab",
        left_side,
        right_side,
        precision=lax.Precision.HIGHEST,
        preferred_element_type=jnp.float32,
    )


def shards(hidden, grad_out, proj_in, proj_out):
    seqs_here = hidden.shape[0]
    length = hidden.shape[1]
    width = proj_in.shape[0]
    inv_root = 1.0 / math.sqrt(length)
    in_panel = jnp.einsum("stf,af->sta", hidden, proj_in, preferred_element_type=jnp.float32)
    out_panel = jnp.einsum("ste,be->stb", grad_out, proj_out, preferred_element_type=jnp.float32)
    panels = jnp.concatenate([in_panel, out_panel], axis=2)
    summed = lax.psum(panels, "tensor")
    seq_outer = outer_sum(summed, width)
    flat_grads = (seq_outer * inv_root).reshape(seqs_here, width * width)
    total_len = width * width
    col_count = total_len // lax.axis_size("tensor")
    row_count = total_len // lax.axis_size("dp")
    col_begin = lax.axis_index("tensor") * col_count
    row_begin = lax.axis_index("dp") * row_count
    all_seqs = seqs_here * lax.axis_size("dp")
    gathered = lax.all_gather(flat_grads, "dp", axis=0, tiled=True)
    row_part = lax.dynamic_slice_in_dim(gathered, row_begin, row_count, 1)
    col_block = lax.dynamic_slice_in_dim(gathered, col_begin, col_count, 1)
    raw_block = jnp.dot(
        row_part.T, col_block, precision=lax.Precision.HIGHEST, preferred_element_type=jnp.float32
    )
    trace_total = jnp.sum(gathered * gathered)
    damping = 0.5 * trace_total / (all_seqs * total_len)
    row_ids = row_begin + lax.broadcasted_iota(jnp.int32, (row_count, col_count), 0)
    col_ids = col_begin + lax.broadcasted_iota(jnp.int32, (row_count, col_count), 1)
    diagonal = jnp.where(row_ids == col_ids, damping, jnp.float32(0.0))
    return raw_block / all_seqs + diagonal


def solution(mesh):
    placed = (
        P("dp", None, "tensor"),
        P("dp", None, "tensor"),
        P(None, "tensor"),
        P(None, "tensor"),
    )
    return jax.shard_map(
        shards, mesh=mesh, in_specs=placed, out_specs=P("dp", "tensor"), check_vma=False
    )
```

profile of v0, /device:TPU:1, one launch (start us, length us, event | category | flops | bytes accessed | tf_op | source)
XLA Modules:
  0.0 158.4 jit_solution(9999071487780403758)
XLA Ops:
  6.5 0.0 copy-start
  6.5 0.0 all-reduce.2.cloned.1.call-start
  6.5 1.6 %copy-done = bf16[1,1024,1024]{2,1,0:T(8,128)(2,1)S(1)} copy-done((bf16[1,1024,1024]{2,1,0:T(8,128)(2,1)S(1)}, bf16[1,1024,1024]{2,1,0:T(8,128)(2,1)}, u32[]{:S(2)}) %copy-start) | copy-done | bytes 2097176
  8.1 1.7 %fusion.4 = f32[1,1024,64]{1,2,0:T(8,128)S(1)} fusion(bf16[64,1024]{1,0:T(8,128)(2,1)} %param.7, bf16[1,1024,1024]{2,1,0:T(8,128)(2,1)S(1)} %copy-done), kind=kOutput, calls=%fused_computation.4 | convolution fusion | flops 134217728 | bytes 2490368 | tf_op jit(solution)/shard_map/ste,be->stb/dot_general | solution.py:27
  9.8 5.4 %fusion.8 = f32[1,1024,64]{1,2,0:T(8,128)S(1)} fusion(bf16[64,3584]{1,0:T(8,128)(2,1)} %param.6, bf16[1,1024,3584]{2,1,0:T(8,128)(2,1)} %param.4), kind=kOutput, calls=%fused_computation.7 | convolution fusion | flops 469762048 | bytes 8060928 | tf_op jit(solution)/shard_map/stf,af->sta/dot_general | solution.py:26
  15.2 0.9 pad_maximum_fusion
  16.1 0.0 all-reduce.2.cloned.1.call-update
  16.1 79.5 %all-reduce.2.cloned.1.call-done = f32[1,1024,128]{1,2,0:T(8,128)} async-done(((f32[1,1024,128]{1,2,0:T(8,128)}), f32[1,1024,128]{1,2,0:T(8,128)}) %all-reduce.2.cloned.1.call-update) | async-done | bytes 524304 | tf_op jit(solution)/shard_map/psum | solution.py:29
  95.6 1.4 convolution_multiply_fusion.1
  97.0 0.1 reshape.25
  97.1 51.0 %all-gather = f32[32,1,4096]{2,1,0:T(1,128)S(1)} all-gather(f32[1,1,4096]{2,1,0:T(1,128)S(1)} %reshape.25), channel_id=1, replica_groups=mesh['dp'=32,'tensor'=8] {'dp'}, dimensions={0}, use_global_device_ids=true | all-gather | bytes 540672 | tf_op jit(solution)/shard_map/all_gather | solution.py:38
  148.1 1.7 %multiply_reduce_fusion = f32[]{:T(128)} fusion(f32[32,1,4096]{2,1,0:T(1,128)S(1)} %all-gather), kind=kLoop, calls=%fused_computation.10 | loop fusion | flops 262143 | bytes 524292 | tf_op jit(solution)/shard_map/reduce_sum | solution.py:44
  150.5 1.1 fusion.7
  (4 shorter events, 0.1 us)
Async XLA Ops:
  6.5 1.6 %copy-start = (bf16[1,1024,1024]{2,1,0:T(8,128)(2,1)S(1)}, bf16[1,1024,1024]{2,1,0:T(8,128)(2,1)}, u32[]{:S(2)}) copy-start(bf16[1,1024,1024]{2,1,0:T(8,128)(2,1)} %param.5) | copy-start | bytes 6291460
  6.5 89.1 %all-reduce.2.cloned.1.call-start = ((), (), s32[]{:S(2)}) async-start(), calls=%async_computation | async-start | bytes 1048576 | tf_op jit(solution)/shard_map/psum | solution.py:29
Sparse Core Ops, SparseCore 0:
  16.2 79.3 all-reduce.1
where the time goes:
time: 159 us; the launch traced here: 158 us
  waiting for transfers between devices  79.5 us (50%)
  blocking collectives  51 us (32%)
  between operations  14.1 us (9%)
  matrix products  9.61 us (6%)
  other arithmetic  2.55 us (2%)
  local copies, waits for them, and re-layouts  1.72 us (1%)
    psum x1, waiting for transfers between devices, shards(): summed = lax.psum(panels, 'tensor')  79.5 us
    all_gather x1, blocking collectives, shards(): gathered = lax.all_gather(flat_grads, 'dp', axis=0, tiled=True)  51 us
    dot_general x1, matrix products, shards(): jnp.einsum('stf,af->sta', hidden, proj_in, preferred_element_type=jnp.flo...  5.43 us
  transfers between devices with their start and end apart: 1, of which 1 were waited for; matrix products, arithmetic and copies ran while one was open for 0% of the time, Pallas kernels for 0%

commit v1 on v0

v1 whole, which is shorter than its diff:
```python
import math

import jax
import jax.numpy as jnp
from jax import lax
from jax.sharding import Mesh, PartitionSpec as P

DP = ("zh", "y", "c")
TENSOR = ("x", "zl")


def shards(hidden, grad_out, proj_in, proj_out):
    length = hidden.shape[1]
    width = proj_in.shape[0]
    inv_root = 1.0 / math.sqrt(length)
    tensor = lax.axis_size(TENSOR)
    outer_dp = lax.axis_size(("zh", "y"))
    cores = lax.axis_size("c")
    seqs = outer_dp * cores
    t = lax.axis_index(TENSOR)
    d = lax.axis_index(DP)
    core = lax.axis_index("c")
    col_as = width // tensor
    row_as = width // seqs

    in_panel = jnp.einsum("tf,af->ta", hidden[0], proj_in, preferred_element_type=jnp.float32)
    out_panel = jnp.einsum("te,be->tb", grad_out[0], proj_out, preferred_element_type=jnp.float32)
    panels = jnp.concatenate([in_panel, out_panel], axis=1)

    parts = lax.all_to_all(panels.reshape(tensor, length // tensor, 2 * width), TENSOR, 0, 0)
    mine = jnp.sum(parts, axis=0)
    partial = lax.dot_general(
        mine[:, :width], mine[:, width:], (((0,), (0,)), ((), ())),
        precision=lax.Precision.HIGHEST, preferred_element_type=jnp.float32,
    ) * inv_root

    copies = jnp.broadcast_to(partial[None], (tensor, width, width))
    grads = jnp.sum(lax.all_to_all(copies, TENSOR, 0, 0), axis=0)

    pair = lax.all_gather(grads, "c")
    squares = jnp.sum(pair * pair, axis=(1, 2))

    cols = lax.dynamic_slice_in_dim(pair, t * col_as, col_as, 1)
    rows = pair.reshape(cores, outer_dp, cores, row_as, width)
    rows = lax.dynamic_index_in_dim(rows, core, 2, keepdims=False)
    rows = rows.transpose(1, 0, 2, 3)
    cols = jnp.broadcast_to(cols[None], (outer_dp, cores, col_as, width))
    squares = jnp.broadcast_to(squares[None, :, None, None], (outer_dp, cores, 1, width))
    sent = jnp.concatenate([cols, rows, squares], axis=2)
    got = lax.all_to_all(sent, ("zh", "y"), 0, 0)
    got = got.reshape(seqs, col_as + row_as + 1, width)
    col_block = got[:, :col_as].reshape(seqs, col_as * width)
    row_block = got[:, col_as:col_as + row_as].reshape(seqs, row_as * width)
    trace_total = jnp.sum(got[:, col_as + row_as, 0])

    raw_block = lax.dot_general(
        row_block, col_block, (((0,), (0,)), ((), ())),
        precision=lax.Precision.HIGHEST, preferred_element_type=jnp.float32,
    )
    total_len = width * width
    damping = 0.5 * trace_total / (seqs * total_len)
    row_count, col_count = raw_block.shape
    row_ids = d * row_count + lax.broadcasted_iota(jnp.int32, (row_count, col_count), 0)
    col_ids = t * col_count + lax.broadcasted_iota(jnp.int32, (row_count, col_count), 1)
    return raw_block / seqs + jnp.where(row_ids == col_ids, damping, jnp.float32(0.0))


def solution(mesh):
    fine = Mesh(mesh.devices.reshape(4, 4, 2, 4, 2), ("zh", "y", "c", "x", "zl"))
    placed = (
        P(DP, None, TENSOR),
        P(DP, None, TENSOR),
        P(None, TENSOR),
        P(None, TENSOR),
    )
    return jax.shard_map(
        shards, mesh=fine, in_specs=placed, out_specs=P(DP, TENSOR), check_vma=False
    )
```

time: 159 us -> 64.7 us (0.41)
  waiting for transfers between devices: 79.5 us -> 14.5 us
  blocking collectives: 51 us -> 19.7 us
  starting transfers between devices: 0.01 us -> 13.4 us
  between operations: 14.1 us -> 0.85 us
  local copies, waits for them, and re-layouts: 1.72 us -> 4.67 us
    psum x1 -> x0, waiting for transfers between devices: 79.5 us -> none  [shards(): summed = lax.psum(panels, 'tensor')]
    all_gather x1, blocking collectives: 51 us -> 4.52 us  [shards(): pair = lax.all_gather(grads, 'c')]
    all_to_all x0 -> x1, blocking collectives: none -> 15.2 us  [shards(): lax.all_to_all(panels.reshape(tensor, length // tensor, 2 * width), TENSO...]
    all_to_all x0 -> x2, waiting for transfers between devices: none -> 14.5 us  [the longest x1 9.01 us: shards(): got = lax.all_to_all(sent, ('zh', 'y'), 0, 0)]
    all_to_all x0 -> x2, starting transfers between devices: none -> 13.4 us  [the longest x1 10 us: shards(): got = lax.all_to_all(sent, ('zh', 'y'), 0, 0)]
    all_to_all x0 -> x2, other arithmetic: none -> 1.89 us  [the longest x1 0.99 us: shards(): grads = jnp.sum(lax.all_to_all(copies, TENSOR, 0, 0), axis=0)]
    unnamed x3 -> x6, local copies, waits for them, and re-layouts: 1.67 us -> 3.51 us
  transfers between devices with their start and end apart: 1 -> 2, of which waited for: 1 -> 2; matrix products, arithmetic and copies ran while one was open for 0% -> 0% of each run, Pallas kernels for 0% -> 0%
where the time goes in v1:
time: 64.7 us; the launch traced here: 64.3 us
  blocking collectives  19.7 us (30%)
  waiting for transfers between devices  14.5 us (22%)
  starting transfers between devices  13.4 us (21%)
  matrix products  8.41 us (13%)
  local copies, waits for them, and re-layouts  4.67 us (7%)
  other arithmetic  2.81 us (4%)
  between operations  0.85 us (1%)
    all_to_all x1, blocking collectives, shards(): lax.all_to_all(panels.reshape(tensor, length // tensor, 2 * width), TENSO...  15.2 us
    all_to_all x1, starting transfers between devices, shards(): got = lax.all_to_all(sent, ('zh', 'y'), 0, 0)  10 us
    all_to_all x1, waiting for transfers between devices, shards(): got = lax.all_to_all(sent, ('zh', 'y'), 0, 0)  9.01 us
    all_to_all x1, waiting for transfers between devices, shards(): grads = jnp.sum(lax.all_to_all(copies, TENSOR, 0, 0), axis=0)  5.46 us
    dot_general x1, matrix products, shards(): jnp.einsum('tf,af->ta', hidden[0], proj_in, preferred_element_type=jnp.fl...  5.43 us
    all_gather x1, blocking collectives, shards(): pair = lax.all_gather(grads, 'c')  4.52 us
    unnamed x6, local copies, waits for them, and re-layouts  3.51 us
    all_to_all x1, starting transfers between devices, shards(): grads = jnp.sum(lax.all_to_all(copies, TENSOR, 0, 0), axis=0)  3.37 us
  transfers between devices with their start and end apart: 2, of which 2 were waited for; matrix products, arithmetic and copies ran while one was open for 0% of the time, Pallas kernels for 0%

profile of v1, /device:TPU:1, one launch (start us, length us, event | category | flops | bytes accessed | tf_op | source)
XLA Modules:
  0.0 64.3 jit_solution(1461621268168857427)
XLA Ops:
  0.0 0.0 copy-start
  0.0 1.6 %copy-done = bf16[1,1024,1024]{2,1,0:T(8,128)(2,1)S(1)} copy-done((bf16[1,1024,1024]{2,1,0:T(8,128)(2,1)S(1)}, bf16[1,1024,1024]{2,1,0:T(8,128)(2,1)}, u32[]{:S(2)}) %copy-start) | copy-done | bytes 2097176
  1.6 1.7 %fusion.2 = f32[1024,64]{0,1:T(8,128)S(1)} fusion(bf16[64,1024]{1,0:T(8,128)(2,1)} %param.7, bf16[1,1024,1024]{2,1,0:T(8,128)(2,1)S(1)} %copy-done), kind=kOutput, calls=%fused_computation.2 | convolution fusion | flops 134217728 | bytes 2490368 | tf_op jit(solution)/shard_map/te,be->tb/dot_general | solution.py:27
  3.3 5.4 %fusion = f32[1024,64]{0,1:T(8,128)S(1)} fusion(bf16[64,3584]{1,0:T(8,128)(2,1)} %param.6, bf16[1,1024,3584]{2,1,0:T(8,128)(2,1)} %param.4), kind=kOutput, calls=%fused_computation | convolution fusion | flops 469762048 | bytes 8060928 | tf_op jit(solution)/shard_map/tf,af->ta/dot_general | solution.py:26
  8.7 15.2 %all_to_all.15 = f32[8,128,128]{1,2,0:T(8,128)S(1)} all-to-all(f32[8,128,128]{1,2,0:T(8,128)S(1)} %copy_bitcast_fusion), channel_id=1, replica_groups=mesh['zh'=4,'y'=4,'c'=2,'x'=4,'zl'=2] {'x','zl'}, dimensions={0} | all-to-all | bytes 1048576 | tf_op jit(solution)/shard_map/all_to_all | solution.py:30
  24.0 0.2 convolution_multiply_fusion.1
  24.2 0.8 %reshape.27 = f32[8,1,4096]{2,1,0:T(1,128)} reshape(f32[8,64,64]{2,1,0:T(8,128)S(1)} %broadcast_in_dim.12) | data formatting | bytes 262144
  25.0 3.4 %all-to-all-start.1 = ((f32[8,1,4096]{2,1,0:T(1,128)}), f32[8,1,4096]{2,1,0:T(1,128)S(1)}, u32[]{:S(2)}, u32[]{:S(2)}) async-start(f32[8,1,4096]{2,1,0:T(1,128)} %reshape.27), calls=%async_computation.1 | async-start | bytes 262144 | tf_op jit(solution)/shard_map/all_to_all | solution.py:38
  28.4 5.5 %all-to-all-done.1 = f32[8,1,4096]{2,1,0:T(1,128)S(1)} async-done(((f32[8,1,4096]{2,1,0:T(1,128)}), f32[8,1,4096]{2,1,0:T(1,128)S(1)}, u32[]{:S(2)}, u32[]{:S(2)}) %all-to-all-start.1) | async-done | bytes 131104 | tf_op jit(solution)/shard_map/all_to_all | solution.py:38
  33.9 0.6 broadcast.9
  34.5 1.0 %reduce.1 = f32[8,4096]{1,0:T(8,128)S(1)} reduce(f32[8,1,4096]{2,1,0:T(1,128)S(1)} %all-to-all-done.1, f32[]{:T(128)} %broadcast.9), dimensions={1}, to_apply=%all_to_all.10.reduce_sub_computation | reduce | bytes 262148 | tf_op jit(solution)/shard_map/all_to_all | solution.py:38
  35.5 0.1 reshape.28
  35.6 4.5 %all-gather = f32[128,64]{1,0:T(8,128)S(1)} all-gather(f32[64,64]{1,0:T(8,128)S(1)} %reduce_sum.37), channel_id=2, replica_groups=mesh['zh'=4,'y'=4,'c'=2,'x'=4,'zl'=2] {'c'}, dimensions={0}, use_global_device_ids=true | all-gather | bytes 49152 | tf_op jit(solution)/shard_map/all_gather | solution.py:40
  40.1 0.1 multiply_reduce_fusion
  40.4 0.1 broadcast_in_dim.28
  40.5 0.1 fusion.7
  40.6 0.8 %reshape.29 = f32[16,1,1408]{2,1,0:T(1,128)} reshape(f32[16,11,2,64]{3,2,1,0:T(2,128)S(1)} %fusion.7) | data formatting | bytes 180224
  41.4 10.0 %all-to-all-start.2 = ((f32[16,1,1408]{2,1,0:T(1,128)}), f32[16,1,1408]{2,1,0:T(1,128)S(1)}, u32[]{:S(2)}, u32[]{:S(2)}) async-start(f32[16,1,1408]{2,1,0:T(1,128)} %reshape.29), calls=%async_computation.2 | async-start | bytes 180224 | tf_op jit(solution)/shard_map/all_to_all | solution.py:50
  51.5 9.0 %all-to-all-done.2 = f32[16,1,1408]{2,1,0:T(1,128)S(1)} async-done(((f32[16,1,1408]{2,1,0:T(1,128)}), f32[16,1,1408]{2,1,0:T(1,128)S(1)}, u32[]{:S(2)}, u32[]{:S(2)}) %all-to-all-start.2) | async-done | bytes 90144 | tf_op jit(solution)/shard_map/all_to_all | solution.py:50
  60.5 0.9 %reduce.2 = f32[16,1408]{1,0:T(8,128)S(1)} reduce(f32[16,1,1408]{2,1,0:T(1,128)S(1)} %all-to-all-done.2, f32[]{:T(128)} %broadcast.9), dimensions={1}, to_apply=%all_to_all.11.reduce_sub_computation | reduce | bytes 180228 | tf_op jit(solution)/shard_map/all_to_all | solution.py:50
  61.4 0.2 reshape.30
  61.5 0.1 copy.32
  61.6 0.6 slice_reduce_fusion
  62.3 0.1 reshape.23
  62.4 0.1 copy.34
  62.4 0.1 reshape.24
  63.2 1.1 %fusion.4 = f32[128,512]{1,0:T(8,128)} fusion(f32[32,128]{1,0:T(8,128)S(1)} %reshape.23, f32[32,512]{1,0:T(8,128)S(1)} %reshape.24, f32[]{:T(128)S(6)} %div.11, s32[512]{0:T(512)S(1)} %iota_add_fusion, s32[128]{0:T(128)S(1)} %iota_add_fusion.1), kind=kOutput, calls=%fused_computation.5 | convolution fusion | flops 25427968 | bytes 346628 | tf_op jit(solution)/shard_map/dot_general | solution.py:56
  (15 shorter events, 0.3 us)
Async XLA Ops:
  0.0 1.6 %copy-start = (bf16[1,1024,1024]{2,1,0:T(8,128)(2,1)S(1)}, bf16[1,1024,1024]{2,1,0:T(8,128)(2,1)}, u32[]{:S(2)}) copy-start(bf16[1,1024,1024]{2,1,0:T(8,128)(2,1)} %param.5) | copy-start | bytes 6291460
  25.0 8.9 %all-to-all-start.1 = ((f32[8,1,4096]{2,1,0:T(1,128)}), f32[8,1,4096]{2,1,0:T(1,128)S(1)}, u32[]{:S(2)}, u32[]{:S(2)}) async-start(f32[8,1,4096]{2,1,0:T(1,128)} %reshape.27), calls=%async_computation.1 | async-start | bytes 262144 | tf_op jit(solution)/shard_map/all_to_all | solution.py:38
  41.4 19.1 %all-to-all-start.2 = ((f32[16,1,1408]{2,1,0:T(1,128)}), f32[16,1,1408]{2,1,0:T(1,128)S(1)}, u32[]{:S(2)}, u32[]{:S(2)}) async-start(f32[16,1,1408]{2,1,0:T(1,128)} %reshape.29), calls=%async_computation.2 | async-start | bytes 180224 | tf_op jit(solution)/shard_map/all_to_all | solution.py:50

commit v2 on v1

v2 whole, which is shorter than its diff:
```python
import functools
import math

import jax
import jax.numpy as jnp
from jax import lax
from jax.experimental import pallas as pl
from jax.experimental.pallas import tpu as pltpu
from jax.sharding import Mesh, PartitionSpec as P

DP = ("zh", "y", "c")
TENSOR = ("x", "zl")
LANES = 128
GRAD_BLOCKS = (1024,)
HIDDEN_BLOCKS = (1024, 1024, 1536)
AHEAD = 2
VMEM_LIMIT = 25165824
F32 = jnp.float32


def panels_kernel(hidden, grad_out, proj_in, proj_out, panels, h_buf, g_buf, p_buf, q_buf, sems, proj_sems):
    width = proj_in.shape[0]
    across = (((1,), (1,)), ((), ()))
    proj_copies = (
        pltpu.make_async_copy(proj_out, q_buf, proj_sems.at[0]),
        pltpu.make_async_copy(proj_in, p_buf, proj_sems.at[1]),
    )
    work = []
    for source, buf, proj, lanes, eighths in (
        (grad_out, g_buf, q_buf, pl.ds(width, width), GRAD_BLOCKS),
        (hidden, h_buf, p_buf, pl.ds(0, width), HIDDEN_BLOCKS),
    ):
        begin = 0
        for size in eighths:
            span = pl.ds(begin, size)
            copy = pltpu.make_async_copy(source.at[:, span], buf.at[:, span], sems.at[len(work)])
            work.append((copy, buf, proj, lanes, span, begin == 0))
            begin += size
        assert begin == source.shape[1]
    for copy in proj_copies:
        copy.start()
    for item in work[:AHEAD]:
        item[0].start()
    for copy in proj_copies:
        copy.wait()
    for k, (copy, buf, proj, lanes, span, first) in enumerate(work):
        copy.wait()
        if k + AHEAD < len(work):
            work[k + AHEAD][0].start()
        part = lax.dot_general(buf[:, span], proj[:, span], across, preferred_element_type=F32)
        panels[:, lanes] = part if first else panels[:, lanes] + part


def make_panels(hidden, grad_out, proj_in, proj_out):
    length, units = hidden.shape
    features = grad_out.shape[1]
    width = proj_in.shape[0]
    blocks = len(GRAD_BLOCKS) + len(HIDDEN_BLOCKS)
    hbm = pl.BlockSpec(memory_space=pltpu.HBM)
    return pl.pallas_call(
        panels_kernel,
        out_shape=jax.ShapeDtypeStruct((length, 2 * width), F32),
        in_specs=[hbm] * 4,
        out_specs=pl.BlockSpec(memory_space=pltpu.VMEM),
        scratch_shapes=[
            pltpu.VMEM((length, units), jnp.bfloat16),
            pltpu.VMEM((length, features), jnp.bfloat16),
            pltpu.VMEM((width, units), jnp.bfloat16),
            pltpu.VMEM((width, features), jnp.bfloat16),
            pltpu.SemaphoreType.DMA((blocks,)),
            pltpu.SemaphoreType.DMA((2,)),
        ],
        compiler_params=pltpu.CompilerParams(vmem_limit_bytes=VMEM_LIMIT),
        name="panels",
    )(hidden, grad_out, proj_in, proj_out)


def outer_kernel(parts, copies, square, *, scale):
    width = square.shape[0]
    mine = jnp.sum(parts[...], axis=0)
    square[...] = lax.dot_general(
        mine[:, :width], mine[:, width:], (((0,), (0,)), ((), ())),
        precision=lax.Precision.HIGHEST, preferred_element_type=F32,
    ) * scale
    half = width // 2
    flat = jnp.concatenate([square[pl.ds(0, half, stride=2), :], square[pl.ds(1, half, stride=2), :]], axis=1)
    for k in range(copies.shape[0]):
        copies[k] = flat


def make_outer(parts, width, receivers, scale):
    return pl.pallas_call(
        functools.partial(outer_kernel, scale=scale),
        out_shape=jax.ShapeDtypeStruct((receivers, width // 2, 2 * width), F32),
        in_specs=[pl.BlockSpec(memory_space=pltpu.VMEM)],
        out_specs=pl.BlockSpec(memory_space=pltpu.VMEM),
        scratch_shapes=[pltpu.VMEM((width, width), F32)],
        compiler_params=pltpu.CompilerParams(vmem_limit_bytes=8 << 20),
        name="outer",
    )(parts)


def pack_kernel(partial, sent, grads, *, tensor, cores, col_rows):
    t = lax.axis_index(TENSOR).astype(jnp.int32)
    core = lax.axis_index("c").astype(jnp.int32)
    chips = sent.shape[0]
    for c in range(cores):
        g = partial[c]
        for k in range(1, tensor):
            g = g + partial[k * cores + c]
        grads[c] = g
        total = jnp.broadcast_to(jnp.sum(g * g), (1, LANES))
        cols = grads[c, pl.ds(t * col_rows, col_rows), :]
        for k in range(chips):
            sent[k, pl.ds(8 * c, col_rows), :] = cols
            sent[k, pl.ds(8 * c + col_rows, 1), :] = grads[c, pl.ds(k * cores + core, 1), :]
            sent[k, pl.ds(8 * c + col_rows + 1, 1), :] = total


def make_sent(partial, tensor, cores, chips, col_rows):
    rows = partial.shape[1]
    return pl.pallas_call(
        functools.partial(pack_kernel, tensor=tensor, cores=cores, col_rows=col_rows),
        out_shape=jax.ShapeDtypeStruct((chips, 8 * cores, LANES), F32),
        in_specs=[pl.BlockSpec(memory_space=pltpu.VMEM)],
        out_specs=pl.BlockSpec(memory_space=pltpu.VMEM),
        scratch_shapes=[pltpu.VMEM((cores, rows, LANES), F32)],
        compiler_params=pltpu.CompilerParams(vmem_limit_bytes=8 << 20),
        name="pack",
    )(partial)


def cov_kernel(got, out, *, col_rows, seqs, total_len):
    row_begin = lax.axis_index(DP).astype(jnp.int32) * out.shape[0]
    col_begin = lax.axis_index(TENSOR).astype(jnp.int32) * out.shape[1]
    cols = jnp.concatenate([got[pl.ds(q, seqs, stride=8), :] for q in range(col_rows)], axis=1)
    rows = got[pl.ds(col_rows, seqs, stride=8), :]
    totals = got[pl.ds(col_rows + 1, seqs, stride=8), :]
    damping = (0.5 / (seqs * total_len)) * jnp.sum(totals, axis=0, keepdims=True)[:, :1]
    raw = lax.dot_general(
        rows, cols, (((0,), (0,)), ((), ())), precision=lax.Precision.HIGHEST, preferred_element_type=F32
    ) * (1.0 / seqs)
    row_ids = row_begin + lax.broadcasted_iota(jnp.int32, raw.shape, 0)
    col_ids = col_begin + lax.broadcasted_iota(jnp.int32, raw.shape, 1)
    out[...] = raw + jnp.where(row_ids == col_ids, damping, 0.0)


def make_cov(got, col_rows, seqs, total_len):
    return pl.pallas_call(
        functools.partial(cov_kernel, col_rows=col_rows, seqs=seqs, total_len=total_len),
        out_shape=jax.ShapeDtypeStruct((LANES, col_rows * LANES), F32),
        in_specs=[pl.BlockSpec(memory_space=pltpu.VMEM)],
        out_specs=pl.BlockSpec(memory_space=pltpu.VMEM),
        compiler_params=pltpu.CompilerParams(vmem_limit_bytes=8 << 20),
        name="cov",
    )(got)


def shards(hidden, grad_out, proj_in, proj_out):
    length = hidden.shape[1]
    width = proj_in.shape[0]
    total_len = width * width
    tensor = lax.axis_size(TENSOR)
    chips = lax.axis_size(("zh", "y"))
    cores = lax.axis_size("c")
    seqs = chips * cores
    col_rows = total_len // tensor // LANES

    panels = make_panels(*(pltpu.with_memory_space_constraint(v, pltpu.HBM) for v in (hidden[0], grad_out[0], proj_in, proj_out)))
    parts = lax.all_to_all(panels.reshape(tensor, length // tensor, 2 * width), TENSOR, 0, 0)
    copies = make_outer(parts, width, tensor * cores, 1.0 / math.sqrt(length))
    partial = lax.all_to_all(copies, (*TENSOR, "c"), 0, 0)
    sent = make_sent(partial, tensor, cores, chips, col_rows)
    got = lax.all_to_all(sent, ("zh", "y"), 0, 0)
    return make_cov(got.reshape(seqs * 8, LANES), col_rows, seqs, total_len)


def solution(mesh):
    fine = Mesh(mesh.devices.reshape(4, 4, 2, 4, 2), ("zh", "y", "c", "x", "zl"))
    placed = (
        P(DP, None, TENSOR),
        P(DP, None, TENSOR),
        P(None, TENSOR),
        P(None, TENSOR),
    )
    return jax.shard_map(
        shards, mesh=fine, in_specs=placed, out_specs=P(DP, TENSOR), check_vma=False
    )
```

time: 64.7 us -> 53.9 us (0.83)
  blocking collectives: 19.7 us -> 46 us
  waiting for transfers between devices: 14.5 us -> 0 us
  starting transfers between devices: 13.4 us -> 0 us
  matrix products: 8.41 us -> 0 us
  Pallas kernels: 0 us -> 7.64 us
  local copies, waits for them, and re-layouts: 4.67 us -> 0 us
  other arithmetic: 2.81 us -> 0 us
  between operations: 0.85 us -> 0.03 us
    all_to_all x0 -> x2, blocking collectives: none -> 30.8 us  [the longest x1 19.2 us: shards(): got = lax.all_to_all(sent, ('zh', 'y'), 0, 0)]
    all_to_all x2 -> x0, waiting for transfers between devices: 14.5 us -> none  [the longest x1 9.01 us: shards(): got = lax.all_to_all(sent, ('zh', 'y'), 0, 0)]
    all_to_all x2 -> x0, starting transfers between devices: 13.4 us -> none  [the longest x1 10 us: shards(): got = lax.all_to_all(sent, ('zh', 'y'), 0, 0)]
    dot_general x4 -> x0, matrix products: 8.41 us -> none  [the longest x1 5.43 us: shards(): jnp.einsum('tf,af->ta', hidden[0], proj_in, preferred_element_type=jnp.fl...]
    pallas_call x0 -> x4, Pallas kernels: none -> 7.64 us  [the longest x1 6.02 us: make_panels(): pl.pallas_call(panels_kernel, out_shape=jax.ShapeDtypeStruct((length, 2 *...]
    all_gather x1 -> x0, blocking collectives: 4.52 us -> none  [shards(): pair = lax.all_gather(grads, 'c')]
    unnamed x6 -> x0, local copies, waits for them, and re-layouts: 3.51 us -> none
    all_to_all x2 -> x0, other arithmetic: 1.89 us -> none  [the longest x1 0.99 us: shards(): grads = jnp.sum(lax.all_to_all(copies, TENSOR, 0, 0), axis=0)]
  transfers between devices with their start and end apart: 2 -> 0, of which waited for: 2 -> 0; matrix products, arithmetic and copies ran while one was open for 0% -> 0% of each run, Pallas kernels for 0% -> 0%
where the time goes in v2:
time: 53.9 us; the launch traced here: 53.7 us
  blocking collectives  46 us (85%)
  Pallas kernels  7.64 us (14%)
    all_to_all x1, blocking collectives, shards(): got = lax.all_to_all(sent, ('zh', 'y'), 0, 0)  19.2 us
    all_to_all x1, blocking collectives, shards(): lax.all_to_all(panels.reshape(tensor, length // tensor, 2 * width), TENSO...  15.2 us
    all_to_all x1, blocking collectives, shards(): partial = lax.all_to_all(copies, (*TENSOR, 'c'), 0, 0)  11.6 us
    pallas_call x1, Pallas kernels, make_panels(): pl.pallas_call(panels_kernel, out_shape=jax.ShapeDtypeStruct((length, 2 *...  6.02 us
    pallas_call x1, Pallas kernels, make_cov(): pl.pallas_call(functools.partial(cov_kernel, col_rows=col_rows, seqs=seqs...  1.12 us

profile of v2, /device:TPU:1, one launch (start us, length us, event | category | flops | bytes accessed | tf_op | source)
XLA Modules:
  0.0 53.7 jit_solution(5376351401187455517)
XLA Ops:
  0.0 6.0 %panels.1 = f32[1024,128]{1,0:T(8,128)S(1)} custom-call(bf16[1024,3584]{1,0:T(8,128)(2,1)} %bitcast.6, bf16[1024,1024]{1,0:T(8,128)(2,1)} %bitcast.7, bf16[64,3584]{1,0:T(8,128)(2,1)} %proj_in.1, bf16[64,1024]{1,0:T(8,128)(2,1)} %proj_out.1), custom_call_target="tpu_custom_call" | custom-call | tf_op jit(solution)/shard_map/panels/pallas_call | solution.py:60
  6.0 15.2 %all_to_all.15.parts = f32[8,128,128]{2,1,0:T(8,128)S(1)} all-to-all(f32[8,128,128]{2,1,0:T(8,128)S(1)} %bitcast.4), channel_id=1, replica_groups=mesh['zh'=4,'y'=4,'c'=2,'x'=4,'zl'=2] {'x','zl'}, dimensions={0} | all-to-all | bytes 1048576 | tf_op jit(solution)/shard_map/all_to_all | solution.py:170
  21.3 0.4 outer.1
  21.6 11.6 %all_to_all.16.partial = f32[16,32,128]{2,1,0:T(8,128)S(1)} all-to-all(f32[16,32,128]{2,1,0:T(8,128)S(1)} %outer.1), channel_id=1, replica_groups=mesh['zh'=4,'y'=4,'c'=2,'x'=4,'zl'=2] {'x','zl','c'}, dimensions={0} | all-to-all | bytes 524288 | tf_op jit(solution)/shard_map/all_to_all | solution.py:172
  33.2 0.1 pack.1
  33.4 19.2 %all_to_all.17 = f32[16,16,128]{2,1,0:T(8,128)S(1)} all-to-all(f32[16,16,128]{2,1,0:T(8,128)S(1)} %pack.1), channel_id=1, replica_groups=mesh['zh'=4,'y'=4,'c'=2,'x'=4,'zl'=2] {'zh','y'}, dimensions={0} | all-to-all | bytes 262144 | tf_op jit(solution)/shard_map/all_to_all | solution.py:174
  52.5 1.1 %cov.1 = f32[128,512]{1,0:T(8,128)} custom-call(f32[256,128]{1,0:T(8,128)S(1)} %bitcast.5), custom_call_target="tpu_custom_call" | custom-call | tf_op jit(solution)/shard_map/cov/pallas_call | solution.py:149

commit v3 on v2

--- a/solution.py
+++ b/solution.py
@@ -11,9 +11,10 @@
 DP = ("zh", "y", "c")
 TENSOR = ("x", "zl")
 LANES = 128
-GRAD_BLOCKS = (1024,)
-HIDDEN_BLOCKS = (1024, 1024, 1536)
-AHEAD = 2
+GRAD_BLOCKS = (512, 512)
+HIDDEN_BLOCKS = (1536, 1024, 1024)
+AHEAD = 3
+ROWS = 256
 VMEM_LIMIT = 25165824
 F32 = jnp.float32
 
@@ -47,8 +48,10 @@
         copy.wait()
         if k + AHEAD < len(work):
             work[k + AHEAD][0].start()
-        part = lax.dot_general(buf[:, span], proj[:, span], across, preferred_element_type=F32)
-        panels[:, lanes] = part if first else panels[:, lanes] + part
+        for r in range(0, panels.shape[0], ROWS):
+            rows = pl.ds(r, ROWS)
+            part = lax.dot_general(buf[rows, span], proj[:, span], across, preferred_element_type=F32)
+            panels[rows, lanes] = part if first else panels[rows, lanes] + part
 
 
 def make_panels(hidden, grad_out, proj_in, proj_out):
@@ -103,25 +106,32 @@
 def pack_kernel(partial, sent, grads, *, tensor, cores, col_rows):
     t = lax.axis_index(TENSOR).astype(jnp.int32)
     core = lax.axis_index("c").astype(jnp.int32)
-    chips = sent.shape[0]
+    each = slot_rows(cores, col_rows)
+    squares = []
     for c in range(cores):
         g = partial[c]
         for k in range(1, tensor):
             g = g + partial[k * cores + c]
         grads[c] = g
-        total = jnp.broadcast_to(jnp.sum(g * g), (1, LANES))
-        cols = grads[c, pl.ds(t * col_rows, col_rows), :]
-        for k in range(chips):
-            sent[k, pl.ds(8 * c, col_rows), :] = cols
-            sent[k, pl.ds(8 * c + col_rows, 1), :] = grads[c, pl.ds(k * cores + core, 1), :]
-            sent[k, pl.ds(8 * c + col_rows + 1, 1), :] = total
+        squares.append(g * g)
+    fill = each - cores * (col_rows + 1)
+    total = jnp.broadcast_to(jnp.sum(sum(squares)), (fill, LANES))
+    for k in range(sent.shape[0] // each):
+        for c in range(cores):
+            sent[pl.ds(k * each + c * col_rows, col_rows), :] = grads[c, pl.ds(t * col_rows, col_rows), :]
+            sent[pl.ds(k * each + cores * col_rows + c, 1), :] = grads[c, pl.ds(k * cores + core, 1), :]
+        sent[pl.ds((k + 1) * each - fill, fill), :] = total
+
+
+def slot_rows(cores, col_rows):
+    return cores * col_rows + 4
 
 
 def make_sent(partial, tensor, cores, chips, col_rows):
     rows = partial.shape[1]
     return pl.pallas_call(
         functools.partial(pack_kernel, tensor=tensor, cores=cores, col_rows=col_rows),
-        out_shape=jax.ShapeDtypeStruct((chips, 8 * cores, LANES), F32),
+        out_shape=jax.ShapeDtypeStruct((chips * slot_rows(cores, col_rows), LANES), F32),
         in_specs=[pl.BlockSpec(memory_space=pltpu.VMEM)],
         out_specs=pl.BlockSpec(memory_space=pltpu.VMEM),
         scratch_shapes=[pltpu.VMEM((cores, rows, LANES), F32)],
@@ -130,27 +140,41 @@
     )(partial)
 
 
-def cov_kernel(got, out, *, col_rows, seqs, total_len):
+def cov_kernel(got, out, block, sems, *, cores, col_rows, seqs, total_len):
+    each = slot_rows(cores, col_rows)
+    chips = seqs // cores
     row_begin = lax.axis_index(DP).astype(jnp.int32) * out.shape[0]
     col_begin = lax.axis_index(TENSOR).astype(jnp.int32) * out.shape[1]
-    cols = jnp.concatenate([got[pl.ds(q, seqs, stride=8), :] for q in range(col_rows)], axis=1)
-    rows = got[pl.ds(col_rows, seqs, stride=8), :]
-    totals = got[pl.ds(col_rows + 1, seqs, stride=8), :]
-    damping = (0.5 / (seqs * total_len)) * jnp.sum(totals, axis=0, keepdims=True)[:, :1]
-    raw = lax.dot_general(
-        rows, cols, (((0,), (0,)), ((), ())), precision=lax.Precision.HIGHEST, preferred_element_type=F32
-    ) * (1.0 / seqs)
-    row_ids = row_begin + lax.broadcasted_iota(jnp.int32, raw.shape, 0)
-    col_ids = col_begin + lax.broadcasted_iota(jnp.int32, raw.shape, 1)
-    out[...] = raw + jnp.where(row_ids == col_ids, damping, 0.0)
-
-
-def make_cov(got, col_rows, seqs, total_len):
-    return pl.pallas_call(
-        functools.partial(cov_kernel, col_rows=col_rows, seqs=seqs, total_len=total_len),
+
+    def over_seqs(first, step):
+        slots = [got[pl.ds(first + c * step, chips, stride=each), :] for c in range(cores)]
+        return jnp.concatenate(slots, axis=0)
+
+    rows = over_seqs(cores * col_rows, 1)
+    totals = got[pl.ds(cores * (col_rows + 1), chips, stride=each), :]
+    damping = (0.5 / (seqs * total_len)) * jnp.sum(totals, axis=0, keepdims=True)
+    row_ids = row_begin + lax.broadcasted_iota(jnp.int32, (out.shape[0], LANES), 0)
+    lane_ids = col_begin + lax.broadcasted_iota(jnp.int32, (out.shape[0], LANES), 1)
+    copies = []
+    for q in range(col_rows):
+        raw = lax.dot_general(
+            rows, over_seqs(q, col_rows), (((0,), (0,)), ((), ())),
+            precision=lax.Precision.HIGHEST, preferred_element_type=F32,
+        )
+        block[q] = raw * (1.0 / seqs) + jnp.where(row_ids == lane_ids + q * LANES, damping, 0.0)
+        copies.append(pltpu.make_async_copy(block.at[q], out.at[:, pl.ds(q * LANES, LANES)], sems.at[q]))
+        copies[q].start()
+    for copy in copies:
+        copy.wait()
+
+
+def make_cov(got, cores, col_rows, seqs, total_len):
+    return pl.pallas_call(
+        functools.partial(cov_kernel, cores=cores, col_rows=col_rows, seqs=seqs, total_len=total_len),
         out_shape=jax.ShapeDtypeStruct((LANES, col_rows * LANES), F32),
         in_specs=[pl.BlockSpec(memory_space=pltpu.VMEM)],
-        out_specs=pl.BlockSpec(memory_space=pltpu.VMEM),
+        out_specs=pl.BlockSpec(memory_space=pltpu.HBM),
+        scratch_shapes=[pltpu.VMEM((col_rows, LANES, LANES), F32), pltpu.SemaphoreType.DMA((col_rows,))],
         compiler_params=pltpu.CompilerParams(vmem_limit_bytes=8 << 20),
         name="cov",
     )(got)
@@ -165,14 +189,15 @@
     cores = lax.axis_size("c")
     seqs = chips * cores
     col_rows = total_len // tensor // LANES
+    each = slot_rows(cores, col_rows)
 
     panels = make_panels(*(pltpu.with_memory_space_constraint(v, pltpu.HBM) for v in (hidden[0], grad_out[0], proj_in, proj_out)))
     parts = lax.all_to_all(panels.reshape(tensor, length // tensor, 2 * width), TENSOR, 0, 0)
     copies = make_outer(parts, width, tensor * cores, 1.0 / math.sqrt(length))
     partial = lax.all_to_all(copies, (*TENSOR, "c"), 0, 0)
     sent = make_sent(partial, tensor, cores, chips, col_rows)
-    got = lax.all_to_all(sent, ("zh", "y"), 0, 0)
-    return make_cov(got.reshape(seqs * 8, LANES), col_rows, seqs, total_len)
+    got = lax.all_to_all(sent.reshape(chips, each // 4, 4, LANES), ("zh", "y"), 0, 0)
+    return make_cov(got.reshape(chips * each, LANES), cores, col_rows, seqs, total_len)
 
 
 def solution(mesh):

time: 53.9 us -> 52.7 us (0.978)
  Pallas kernels: 7.64 us -> 6.72 us
    pallas_call x1, Pallas kernels: 6.02 us -> 5.12 us  [make_panels(): pl.pallas_call(panels_kernel, out_shape=jax.ShapeDtypeStruct((length, 2 *...]
where the time goes in v3:
time: 52.7 us; the launch traced here: 52.5 us
  blocking collectives  45.7 us (87%)
  Pallas kernels  6.72 us (13%)
    all_to_all x1, blocking collectives, shards(): lax.all_to_all(sent.reshape(chips, each // 4, 4, LANES), ('zh', 'y'), 0, 0)  18.9 us
    all_to_all x1, blocking collectives, shards(): lax.all_to_all(panels.reshape(tensor, length // tensor, 2 * width), TENSO...  15.2 us
    all_to_all x1, blocking collectives, shards(): partial = lax.all_to_all(copies, (*TENSOR, 'c'), 0, 0)  11.6 us
    pallas_call x1, Pallas kernels, make_panels(): pl.pallas_call(panels_kernel, out_shape=jax.ShapeDtypeStruct((length, 2 *...  5.12 us
    pallas_call x1, Pallas kernels, make_cov(): pl.pallas_call(functools.partial(cov_kernel, cores=cores, col_rows=col_ro...  1.1 us

profile of v3, /device:TPU:1, one launch (start us, length us, event | category | flops | bytes accessed | tf_op | source)
XLA Modules:
  0.0 52.5 jit_solution(6035039966964035205)
XLA Ops:
  0.0 5.1 %panels.1 = f32[1024,128]{1,0:T(8,128)S(1)} custom-call(bf16[1024,3584]{1,0:T(8,128)(2,1)} %bitcast.8, bf16[1024,1024]{1,0:T(8,128)(2,1)} %bitcast.9, bf16[64,3584]{1,0:T(8,128)(2,1)} %proj_in.1, bf16[64,1024]{1,0:T(8,128)(2,1)} %proj_out.1), custom_call_target="tpu_custom_call" | custom-call | tf_op jit(solution)/shard_map/panels/pallas_call | solution.py:63
  5.1 15.2 %all_to_all.15.parts = f32[8,128,128]{2,1,0:T(8,128)S(1)} all-to-all(f32[8,128,128]{2,1,0:T(8,128)S(1)} %bitcast.5), channel_id=1, replica_groups=mesh['zh'=4,'y'=4,'c'=2,'x'=4,'zl'=2] {'x','zl'}, dimensions={0} | all-to-all | bytes 1048576 | tf_op jit(solution)/shard_map/all_to_all | solution.py:195
  20.3 0.4 outer.1
  20.7 11.6 %all_to_all.16.partial = f32[16,32,128]{2,1,0:T(8,128)S(1)} all-to-all(f32[16,32,128]{2,1,0:T(8,128)S(1)} %outer.1), channel_id=1, replica_groups=mesh['zh'=4,'y'=4,'c'=2,'x'=4,'zl'=2] {'x','zl','c'}, dimensions={0} | all-to-all | bytes 524288 | tf_op jit(solution)/shard_map/all_to_all | solution.py:197
  32.3 0.1 pack.1
  32.5 18.9 %all_to_all.17 = f32[16,3,4,128]{3,2,1,0:T(4,128)S(1)} all-to-all(f32[16,3,4,128]{3,2,1,0:T(4,128)S(1)} %bitcast.6), channel_id=1, replica_groups=mesh['zh'=4,'y'=4,'c'=2,'x'=4,'zl'=2] {'zh','y'}, dimensions={0} | all-to-all | bytes 196608 | tf_op jit(solution)/shard_map/all_to_all | solution.py:199
  51.4 1.1 %cov.1 = f32[128,512]{1,0:T(8,128)} custom-call(f32[192,128]{1,0:T(8,128)S(1)} %bitcast.7), custom_call_target="tpu_custom_call" | custom-call | tf_op jit(solution)/shard_map/cov/pallas_call | solution.py:172

commit v4 on v3

--- a/solution.py
+++ b/solution.py
@@ -8,9 +8,11 @@
 from jax.experimental.pallas import tpu as pltpu
 from jax.sharding import Mesh, PartitionSpec as P
 
-DP = ("zh", "y", "c")
-TENSOR = ("x", "zl")
+DP = ("p", "c")
+TENSOR = "t"
 LANES = 128
+P_ORDER = [10, 0, 1, 3, 2, 4, 5, 7, 6, 12, 8, 13, 15, 14, 9, 11]
+T_ORDER = [5, 7, 4, 3, 6, 2, 1, 0]
 GRAD_BLOCKS = (512, 512)
 HIDDEN_BLOCKS = (1536, 1024, 1024)
 AHEAD = 3
@@ -119,7 +121,7 @@
     for k in range(sent.shape[0] // each):
         for c in range(cores):
             sent[pl.ds(k * each + c * col_rows, col_rows), :] = grads[c, pl.ds(t * col_rows, col_rows), :]
-            sent[pl.ds(k * each + cores * col_rows + c, 1), :] = grads[c, pl.ds(k * cores + core, 1), :]
+            sent[pl.ds(k * each + cores * col_rows + c, 1), :] = grads[c, pl.ds(P_ORDER[k] * cores + core, 1), :]
         sent[pl.ds((k + 1) * each - fill, fill), :] = total
 
 
@@ -185,23 +187,23 @@
     width = proj_in.shape[0]
     total_len = width * width
     tensor = lax.axis_size(TENSOR)
-    chips = lax.axis_size(("zh", "y"))
+    chips = lax.axis_size("p")
     cores = lax.axis_size("c")
     seqs = chips * cores
     col_rows = total_len // tensor // LANES
     each = slot_rows(cores, col_rows)
 
     panels = make_panels(*(pltpu.with_memory_space_constraint(v, pltpu.HBM) for v in (hidden[0], grad_out[0], proj_in, proj_out)))
-    parts = lax.all_to_all(panels.reshape(tensor, length // tensor, 2 * width), TENSOR, 0, 0)
+    parts = lax.all_to_all(panels.reshape(tensor, length // tensor, 2 * width), TENSOR, 0, 0, axis_index_groups=[T_ORDER])
     copies = make_outer(parts, width, tensor * cores, 1.0 / math.sqrt(length))
-    partial = lax.all_to_all(copies, (*TENSOR, "c"), 0, 0)
+    partial = lax.all_to_all(copies, (TENSOR, "c"), 0, 0)
     sent = make_sent(partial, tensor, cores, chips, col_rows)
-    got = lax.all_to_all(sent.reshape(chips, each // 4, 4, LANES), ("zh", "y"), 0, 0)
+    got = lax.all_to_all(sent.reshape(chips, each // 4, 4, LANES), "p", 0, 0, axis_index_groups=[P_ORDER])
     return make_cov(got.reshape(chips * each, LANES), cores, col_rows, seqs, total_len)
 
 
 def solution(mesh):
-    fine = Mesh(mesh.devices.reshape(4, 4, 2, 4, 2), ("zh", "y", "c", "x", "zl"))
+    fine = Mesh(mesh.devices.reshape(16, 2, 8), ("p", "c", "t"))
     placed = (
         P(DP, None, TENSOR),
         P(DP, None, TENSOR),

time: 52.7 us -> 48.2 us (0.915)
  blocking collectives: 45.7 us -> 40.9 us
    all_to_all x2, blocking collectives: 30.5 us -> 28 us  [the longest x1 14 us: shards(): lax.all_to_all(sent.reshape(chips, each // 4, 4, LANES), 'p', 0, 0, axis_...]
    all_to_all x1, blocking collectives: 15.2 us -> 12.8 us  [shards(): lax.all_to_all(panels.reshape(tensor, length // tensor, 2 * width), TENSO...]
where the time goes in v4:
time: 48.2 us; the launch traced here: 47.6 us
  blocking collectives  40.9 us (85%)
  Pallas kernels  6.72 us (14%)
    all_to_all x1, blocking collectives, shards(): lax.all_to_all(sent.reshape(chips, each // 4, 4, LANES), 'p', 0, 0, axis_...  14 us
    all_to_all x1, blocking collectives, shards(): partial = lax.all_to_all(copies, (TENSOR, 'c'), 0, 0)  14 us
    all_to_all x1, blocking collectives, shards(): lax.all_to_all(panels.reshape(tensor, length // tensor, 2 * width), TENSO...  12.8 us
    pallas_call x1, Pallas kernels, make_panels(): pl.pallas_call(panels_kernel, out_shape=jax.ShapeDtypeStruct((length, 2 *...  5.12 us
    pallas_call x1, Pallas kernels, make_cov(): pl.pallas_call(functools.partial(cov_kernel, cores=cores, col_rows=col_ro...  1.1 us

profile of v4, /device:TPU:1, one launch (start us, length us, event | category | flops | bytes accessed | tf_op | source)
XLA Modules:
  0.0 47.6 jit_solution(4087945183073664067)
XLA Ops:
  0.0 5.1 %panels.1 = f32[1024,128]{1,0:T(8,128)S(1)} custom-call(bf16[1024,3584]{1,0:T(8,128)(2,1)} %bitcast.8, bf16[1024,1024]{1,0:T(8,128)(2,1)} %bitcast.9, bf16[64,3584]{1,0:T(8,128)(2,1)} %proj_in.1, bf16[64,1024]{1,0:T(8,128)(2,1)} %proj_out.1), custom_call_target="tpu_custom_call" | custom-call | tf_op jit(solution)/shard_map/panels/pallas_call | solution.py:65
  5.1 12.8 %all_to_all.15.parts = f32[8,128,128]{2,1,0:T(8,128)S(1)} all-to-all(f32[8,128,128]{2,1,0:T(8,128)S(1)} %bitcast.5), channel_id=1, replica_groups={{5,7,4,3,6,2,1,0},{13,15,12,11,14,10,9,8},{21,23,20,19,22,18,17,16},{29..., dimensions={0} | all-to-all | bytes 1048576 | tf_op jit(solution)/shard_map/all_to_all | solution.py:197
  18.0 0.4 outer.1
  18.3 14.0 %all_to_all.16.partial = f32[16,32,128]{2,1,0:T(8,128)S(1)} all-to-all(f32[16,32,128]{2,1,0:T(8,128)S(1)} %outer.1), channel_id=1, replica_groups=mesh['p'=16,'c'=2,'t'=8] {'t','c'}, dimensions={0} | all-to-all | bytes 524288 | tf_op jit(solution)/shard_map/all_to_all | solution.py:199
  32.3 0.1 pack.1
  32.5 14.0 %all_to_all.17 = f32[16,3,4,128]{3,2,1,0:T(4,128)S(1)} all-to-all(f32[16,3,4,128]{3,2,1,0:T(4,128)S(1)} %bitcast.6), channel_id=1, replica_groups={{160,0,16,48,32,64,80,112,96,192,128,208,240,224,144,176},{161,1,17,49,..., dimensions={0} | all-to-all | bytes 196608 | tf_op jit(solution)/shard_map/all_to_all | solution.py:201
  46.5 1.1 %cov.1 = f32[128,512]{1,0:T(8,128)} custom-call(f32[192,128]{1,0:T(8,128)S(1)} %bitcast.7), custom_call_target="tpu_custom_call" | custom-call | tf_op jit(solution)/shard_map/cov/pallas_call | solution.py:174

commit v5 on v4

--- a/solution.py
+++ b/solution.py
@@ -13,6 +13,7 @@
 LANES = 128
 P_ORDER = [10, 0, 1, 3, 2, 4, 5, 7, 6, 12, 8, 13, 15, 14, 9, 11]
 T_ORDER = [5, 7, 4, 3, 6, 2, 1, 0]
+A_ORDER = [11, 0, 1, 2, 3, 4, 5, 6, 7, 8, 9, 10, 12, 13, 14, 15]
 GRAD_BLOCKS = (512, 512)
 HIDDEN_BLOCKS = (1536, 1024, 1024)
 AHEAD = 3
@@ -111,9 +112,10 @@
     each = slot_rows(cores, col_rows)
     squares = []
     for c in range(cores):
-        g = partial[c]
-        for k in range(1, tensor):
-            g = g + partial[k * cores + c]
+        mine = [k for k, place in enumerate(A_ORDER) if place % cores == c]
+        g = partial[mine[0]]
+        for k in mine[1:]:
+            g = g + partial[k]
         grads[c] = g
         squares.append(g * g)
     fill = each - cores * (col_rows + 1)
@@ -196,7 +198,7 @@
     panels = make_panels(*(pltpu.with_memory_space_constraint(v, pltpu.HBM) for v in (hidden[0], grad_out[0], proj_in, proj_out)))
     parts = lax.all_to_all(panels.reshape(tensor, length // tensor, 2 * width), TENSOR, 0, 0, axis_index_groups=[T_ORDER])
     copies = make_outer(parts, width, tensor * cores, 1.0 / math.sqrt(length))
-    partial = lax.all_to_all(copies, (TENSOR, "c"), 0, 0)
+    partial = lax.all_to_all(copies, (TENSOR, "c"), 0, 0, axis_index_groups=[A_ORDER])
     sent = make_sent(partial, tensor, cores, chips, col_rows)
     got = lax.all_to_all(sent.reshape(chips, each // 4, 4, LANES), "p", 0, 0, axis_index_groups=[P_ORDER])
     return make_cov(got.reshape(chips * each, LANES), cores, col_rows, seqs, total_len)

time: 48.2 us -> 46 us (0.954)
  blocking collectives: 40.9 us -> 38.5 us
    all_to_all x1, blocking collectives: 14 us -> 11.7 us  [shards(): lax.all_to_all(copies, (TENSOR, 'c'), 0, 0, axis_index_groups=[A_ORDER])]
where the time goes in v5:
time: 46 us; the launch traced here: 45.3 us
  blocking collectives  38.5 us (84%)
  Pallas kernels  6.72 us (15%)
    all_to_all x1, blocking collectives, shards(): lax.all_to_all(sent.reshape(chips, each // 4, 4, LANES), 'p', 0, 0, axis_...  14 us
    all_to_all x1, blocking collectives, shards(): lax.all_to_all(panels.reshape(tensor, length // tensor, 2 * width), TENSO...  12.8 us
    all_to_all x1, blocking collectives, shards(): lax.all_to_all(copies, (TENSOR, 'c'), 0, 0, axis_index_groups=[A_ORDER])  11.7 us
    pallas_call x1, Pallas kernels, make_panels(): pl.pallas_call(panels_kernel, out_shape=jax.ShapeDtypeStruct((length, 2 *...  5.12 us
    pallas_call x1, Pallas kernels, make_cov(): pl.pallas_call(functools.partial(cov_kernel, cores=cores, col_rows=col_ro...  1.1 us

profile of v5, /device:TPU:1, one launch (start us, length us, event | category | flops | bytes accessed | tf_op | source)
XLA Modules:
  0.0 45.3 jit_solution(5641723630249579790)
XLA Ops:
  0.0 5.1 %panels.1 = f32[1024,128]{1,0:T(8,128)S(1)} custom-call(bf16[1024,3584]{1,0:T(8,128)(2,1)} %bitcast.8, bf16[1024,1024]{1,0:T(8,128)(2,1)} %bitcast.9, bf16[64,3584]{1,0:T(8,128)(2,1)} %proj_in.1, bf16[64,1024]{1,0:T(8,128)(2,1)} %proj_out.1), custom_call_target="tpu_custom_call" | custom-call | tf_op jit(solution)/shard_map/panels/pallas_call | solution.py:66
  5.1 12.8 %all_to_all.15.parts = f32[8,128,128]{2,1,0:T(8,128)S(1)} all-to-all(f32[8,128,128]{2,1,0:T(8,128)S(1)} %bitcast.5), channel_id=1, replica_groups={{5,7,4,3,6,2,1,0},{13,15,12,11,14,10,9,8},{21,23,20,19,22,18,17,16},{29..., dimensions={0} | all-to-all | bytes 1048576 | tf_op jit(solution)/shard_map/all_to_all | solution.py:199
  18.0 0.4 outer.1
  18.3 11.7 %all_to_all.16.partial = f32[16,32,128]{2,1,0:T(8,128)S(1)} all-to-all(f32[16,32,128]{2,1,0:T(8,128)S(1)} %outer.1), channel_id=1, replica_groups={{13,0,8,1,9,2,10,3,11,4,12,5,6,14,7,15},{29,16,24,17,25,18,26,19,27,20,..., dimensions={0} | all-to-all | bytes 524288 | tf_op jit(solution)/shard_map/all_to_all | solution.py:201
  30.1 0.1 pack.1
  30.2 14.0 %all_to_all.17 = f32[16,3,4,128]{3,2,1,0:T(4,128)S(1)} all-to-all(f32[16,3,4,128]{3,2,1,0:T(4,128)S(1)} %bitcast.6), channel_id=1, replica_groups={{160,0,16,48,32,64,80,112,96,192,128,208,240,224,144,176},{161,1,17,49,..., dimensions={0} | all-to-all | bytes 196608 | tf_op jit(solution)/shard_map/all_to_all | solution.py:203
  44.2 1.1 %cov.1 = f32[128,512]{1,0:T(8,128)} custom-call(f32[192,128]{1,0:T(8,128)S(1)} %bitcast.7), custom_call_target="tpu_custom_call" | custom-call | tf_op jit(solution)/shard_map/cov/pallas_call | solution.py:176

commit v6 on v5

--- a/solution.py
+++ b/solution.py
@@ -11,7 +11,7 @@
 DP = ("p", "c")
 TENSOR = "t"
 LANES = 128
-P_ORDER = [10, 0, 1, 3, 2, 4, 5, 7, 6, 12, 8, 13, 15, 14, 9, 11]
+P_ORDER = [10, 0, 1, 2, 3, 4, 5, 6, 7, 8, 9, 11, 12, 13, 14, 15]
 T_ORDER = [5, 7, 4, 3, 6, 2, 1, 0]
 A_ORDER = [11, 0, 1, 2, 3, 4, 5, 6, 7, 8, 9, 10, 12, 13, 14, 15]
 GRAD_BLOCKS = (512, 512)
@@ -86,7 +86,7 @@
     mine = jnp.sum(parts[...], axis=0)
     square[...] = lax.dot_general(
         mine[:, :width], mine[:, width:], (((0,), (0,)), ((), ())),
-        precision=lax.Precision.HIGHEST, preferred_element_type=F32,
+        precision=lax.Precision.HIGH, preferred_element_type=F32,
     ) * scale
     half = width // 2
     flat = jnp.concatenate([square[pl.ds(0, half, stride=2), :], square[pl.ds(1, half, stride=2), :]], axis=1)
@@ -163,7 +163,7 @@
     for q in range(col_rows):
         raw = lax.dot_general(
             rows, over_seqs(q, col_rows), (((0,), (0,)), ((), ())),
-            precision=lax.Precision.HIGHEST, preferred_element_type=F32,
+            precision=lax.Precision.HIGH, preferred_element_type=F32,
         )
         block[q] = raw * (1.0 / seqs) + jnp.where(row_ids == lane_ids + q * LANES, damping, 0.0)
         copies.append(pltpu.make_async_copy(block.at[q], out.at[:, pl.ds(q * LANES, LANES)], sems.at[q]))

time: 46 us -> 45.7 us (level)
  no operation moved by 1% of the time
where the time goes in v6:
time: 45.7 us; the launch traced here: 45.4 us
  blocking collectives  38.7 us (85%)
  Pallas kernels  6.59 us (14%)
    all_to_all x1, blocking collectives, shards(): lax.all_to_all(sent.reshape(chips, each // 4, 4, LANES), 'p', 0, 0, axis_...  14.2 us
    all_to_all x1, blocking collectives, shards(): lax.all_to_all(panels.reshape(tensor, length // tensor, 2 * width), TENSO...  12.8 us
    all_to_all x1, blocking collectives, shards(): lax.all_to_all(copies, (TENSOR, 'c'), 0, 0, axis_index_groups=[A_ORDER])  11.7 us
    pallas_call x1, Pallas kernels, make_panels(): pl.pallas_call(panels_kernel, out_shape=jax.ShapeDtypeStruct((length, 2 *...  5.12 us
    pallas_call x1, Pallas kernels, make_cov(): pl.pallas_call(functools.partial(cov_kernel, cores=cores, col_rows=col_ro...  1 us

profile of v6, /device:TPU:1, one launch (start us, length us, event | category | flops | bytes accessed | tf_op | source)
XLA Modules:
  0.0 45.4 jit_solution(13633125869271980452)
XLA Ops:
  0.0 5.1 %panels.1 = f32[1024,128]{1,0:T(8,128)S(1)} custom-call(bf16[1024,3584]{1,0:T(8,128)(2,1)} %bitcast.8, bf16[1024,1024]{1,0:T(8,128)(2,1)} %bitcast.9, bf16[64,3584]{1,0:T(8,128)(2,1)} %proj_in.1, bf16[64,1024]{1,0:T(8,128)(2,1)} %proj_out.1), custom_call_target="tpu_custom_call" | custom-call | tf_op jit(solution)/shard_map/panels/pallas_call | solution.py:66
  5.1 12.8 %all_to_all.15.parts = f32[8,128,128]{2,1,0:T(8,128)S(1)} all-to-all(f32[8,128,128]{2,1,0:T(8,128)S(1)} %bitcast.5), channel_id=1, replica_groups={{5,7,4,3,6,2,1,0},{13,15,12,11,14,10,9,8},{21,23,20,19,22,18,17,16},{29..., dimensions={0} | all-to-all | bytes 1048576 | tf_op jit(solution)/shard_map/all_to_all | solution.py:199
  18.0 0.3 outer.1
  18.3 11.7 %all_to_all.16.partial = f32[16,32,128]{2,1,0:T(8,128)S(1)} all-to-all(f32[16,32,128]{2,1,0:T(8,128)S(1)} %outer.1), channel_id=1, replica_groups={{13,0,8,1,9,2,10,3,11,4,12,5,6,14,7,15},{29,16,24,17,25,18,26,19,27,20,..., dimensions={0} | all-to-all | bytes 524288 | tf_op jit(solution)/shard_map/all_to_all | solution.py:201
  30.0 0.1 pack.1
  30.2 14.2 %all_to_all.17 = f32[16,3,4,128]{3,2,1,0:T(4,128)S(1)} all-to-all(f32[16,3,4,128]{3,2,1,0:T(4,128)S(1)} %bitcast.6), channel_id=1, replica_groups={{160,0,16,32,48,64,80,96,112,128,144,176,192,208,224,240},{161,1,17,33,..., dimensions={0} | all-to-all | bytes 196608 | tf_op jit(solution)/shard_map/all_to_all | solution.py:203
  44.4 1.0 %cov.1 = f32[128,512]{1,0:T(8,128)} custom-call(f32[192,128]{1,0:T(8,128)S(1)} %bitcast.7), custom_call_target="tpu_custom_call" | custom-call | tf_op jit(solution)/shard_map/cov/pallas_call | solution.py:176

commit v7 on v5

--- a/solution.py
+++ b/solution.py
@@ -14,8 +14,8 @@
 P_ORDER = [10, 0, 1, 3, 2, 4, 5, 7, 6, 12, 8, 13, 15, 14, 9, 11]
 T_ORDER = [5, 7, 4, 3, 6, 2, 1, 0]
 A_ORDER = [11, 0, 1, 2, 3, 4, 5, 6, 7, 8, 9, 10, 12, 13, 14, 15]
-GRAD_BLOCKS = (512, 512)
-HIDDEN_BLOCKS = (1536, 1024, 1024)
+GRAD_BLOCKS = (256, 768)
+HIDDEN_BLOCKS = (1536, 1280, 768)
 AHEAD = 3
 ROWS = 256
 VMEM_LIMIT = 25165824

time: 46 us -> 46 us (level)
  no operation moved by 1% of the time
where the time goes in v7:
time: 46 us; the launch traced here: 45.3 us
  blocking collectives  38.5 us (84%)
  Pallas kernels  6.75 us (15%)
    all_to_all x1, blocking collectives, shards(): lax.all_to_all(sent.reshape(chips, each // 4, 4, LANES), 'p', 0, 0, axis_...  14 us
    all_to_all x1, blocking collectives, shards(): lax.all_to_all(panels.reshape(tensor, length // tensor, 2 * width), TENSO...  12.8 us
    all_to_all x1, blocking collectives, shards(): lax.all_to_all(copies, (TENSOR, 'c'), 0, 0, axis_index_groups=[A_ORDER])  11.7 us
    pallas_call x1, Pallas kernels, make_panels(): pl.pallas_call(panels_kernel, out_shape=jax.ShapeDtypeStruct((length, 2 *...  5.15 us
    pallas_call x1, Pallas kernels, make_cov(): pl.pallas_call(functools.partial(cov_kernel, cores=cores, col_rows=col_ro...  1.1 us

profile of v7, /device:TPU:1, one launch (start us, length us, event | category | flops | bytes accessed | tf_op | source)
XLA Modules:
  0.0 45.3 jit_solution(88022527184167935)
XLA Ops:
  0.0 5.1 %panels.1 = f32[1024,128]{1,0:T(8,128)S(1)} custom-call(bf16[1024,3584]{1,0:T(8,128)(2,1)} %bitcast.8, bf16[1024,1024]{1,0:T(8,128)(2,1)} %bitcast.9, bf16[64,3584]{1,0:T(8,128)(2,1)} %proj_in.1, bf16[64,1024]{1,0:T(8,128)(2,1)} %proj_out.1), custom_call_target="tpu_custom_call" | custom-call | tf_op jit(solution)/shard_map/panels/pallas_call | solution.py:66
  5.2 12.8 %all_to_all.15.parts = f32[8,128,128]{2,1,0:T(8,128)S(1)} all-to-all(f32[8,128,128]{2,1,0:T(8,128)S(1)} %bitcast.5), channel_id=1, replica_groups={{5,7,4,3,6,2,1,0},{13,15,12,11,14,10,9,8},{21,23,20,19,22,18,17,16},{29..., dimensions={0} | all-to-all | bytes 1048576 | tf_op jit(solution)/shard_map/all_to_all | solution.py:199
  18.0 0.4 outer.1
  18.4 11.7 %all_to_all.16.partial = f32[16,32,128]{2,1,0:T(8,128)S(1)} all-to-all(f32[16,32,128]{2,1,0:T(8,128)S(1)} %outer.1), channel_id=1, replica_groups={{13,0,8,1,9,2,10,3,11,4,12,5,6,14,7,15},{29,16,24,17,25,18,26,19,27,20,..., dimensions={0} | all-to-all | bytes 524288 | tf_op jit(solution)/shard_map/all_to_all | solution.py:201
  30.1 0.1 pack.1
  30.2 14.0 %all_to_all.17 = f32[16,3,4,128]{3,2,1,0:T(4,128)S(1)} all-to-all(f32[16,3,4,128]{3,2,1,0:T(4,128)S(1)} %bitcast.6), channel_id=1, replica_groups={{160,0,16,48,32,64,80,112,96,192,128,208,240,224,144,176},{161,1,17,49,..., dimensions={0} | all-to-all | bytes 196608 | tf_op jit(solution)/shard_map/all_to_all | solution.py:203
  44.2 1.1 %cov.1 = f32[128,512]{1,0:T(8,128)} custom-call(f32[192,128]{1,0:T(8,128)S(1)} %bitcast.7), custom_call_target="tpu_custom_call" | custom-call | tf_op jit(solution)/shard_map/cov/pallas_call | solution.py:176
